TPU v7x, 512 devices: a whole 4x4x16 slice. The times are simulated.
512 devices in a mesh: gz: 16 (over z), gy: 32 (over x, y, core).
Axes of the slice: x: 4, y: 4, z: 16, core: 2. Of those that a mesh axis runs over, the one named last changes fastest.
Arguments:
- tracer: float32 [512, 1024, 128], P('gz', 'gy'), may hold values from 0.1 to 10
- y_speed: float32 [512, 1024, 128], P('gz', 'gy'), may hold values from -0.4 to 0.4
- z_speed: float32 [512, 1024, 128], P('gz', 'gy'), may hold values from -0.4 to 0.4
- kappa: float32 [512, 1024, 128], P('gz', 'gy'), may hold values from 0.5 to 8
Outputs:
- updated: float32 [512, 1024, 128], P('gz', 'gy')
All inputs are finite; a program needn't handle non-finite values.
Results may differ from a plain program's by a relative error of at most 0.0003.
Values sent between devices are 32-bit elements; how exact they have to be, the bound alone decides.
A program may use at most 64 MiB of HBM per device.

v0:
```python
import jax
import jax.numpy as jnp
from jax import lax
from jax.sharding import PartitionSpec as P

NSUB = 4
rate_const = 500.0


def padded_2(x, sides, width):
    for axis, dim in sides:
        peers, length = (lax.axis_size(axis), x.shape[dim])
        up = [(i, (i + 1) % peers) for i in range(peers - 1)]
        down = [(j, i) for i, j in up]
        last = lax.slice_in_dim(x, length - width, length, axis=dim)
        leading = lax.slice_in_dim(x, 0, width, axis=dim)
        before = lax.ppermute(last, axis, up)
        after = lax.ppermute(leading, axis, down)
        x = jnp.concatenate([before, x, after], axis=dim)
    return x


def from_behind(x, axis, by):
    peers = lax.axis_size(axis)
    pairs = [(i, i + by) for i in range(peers) if 0 <= i + by < peers]
    return lax.ppermute(x, axis, pairs)


def advect_once(tracer, y_speed, z_speed):
    face_y = 0.5 * (y_speed[:, 1:] + y_speed[:, :-1])
    flux_y = jnp.maximum(face_y, 0.0) * tracer[:, :-1] + jnp.minimum(face_y, 0.0) * tracer[:, 1:]
    diff_y = flux_y[:, 1:] - flux_y[:, :-1]
    face_z = 0.5 * (z_speed[1:] + z_speed[:-1])
    flux_z = jnp.maximum(face_z, 0.0) * tracer[:-1] + jnp.minimum(face_z, 0.0) * tracer[1:]
    diff_z = flux_z[1:] - flux_z[:-1]
    return tracer[1:-1, 1:-1] - diff_y[1:-1] - diff_z[:, 1:-1]


def move_down(values, offset, axis, fill):
    count = values.shape[axis]
    kept = lax.slice_in_dim(values, 0, count - offset, axis=axis)
    padding = jnp.full_like(lax.slice_in_dim(values, 0, offset, axis=axis), fill)
    return jnp.concatenate([padding, kept], axis=axis)


def move_up(values, offset, axis, fill):
    count = values.shape[axis]
    kept = lax.slice_in_dim(values, offset, count, axis=axis)
    padding = jnp.full_like(lax.slice_in_dim(values, 0, offset, axis=axis), fill)
    return jnp.concatenate([kept, padding], axis=axis)


def reduce_lines(sub_diag, main_diag, sup_diag, rights, axis):
    count = main_diag.shape[axis]
    offset = 1
    while offset < count:
        factor_low = -sub_diag / move_down(main_diag, offset, axis, 1.0)
        factor_high = -sup_diag / move_up(main_diag, offset, axis, 1.0)
        new_main = (
            main_diag
            + factor_low * move_down(sup_diag, offset, axis, 0.0)
            + factor_high * move_up(sub_diag, offset, axis, 0.0)
        )
        new_sub = factor_low * move_down(sub_diag, offset, axis, 0.0)
        new_sup = factor_high * move_up(sup_diag, offset, axis, 0.0)
        rights = tuple(
            (
                right
                + factor_low * move_down(right, offset, axis, 0.0)
                + factor_high * move_up(right, offset, axis, 0.0)
                for right in rights
            )
        )
        sub_diag, main_diag, sup_diag = (new_sub, new_main, new_sup)
        offset = offset * 2
    return tuple((right / main_diag for right in rights))


def solve_rows(items):
    tracer_part, kappa_part = items
    count = kappa_part.shape[1]
    inner = rate_const * 0.5 * (kappa_part[:, 1:] + kappa_part[:, :-1])
    lower = jnp.concatenate([rate_const * kappa_part[:, :1], inner], axis=1)
    upper = jnp.concatenate([inner, rate_const * kappa_part[:, count - 1 :]], axis=1)
    main_diag = 1.0 + lower + upper
    zero_row = jnp.zeros_like(kappa_part[:, :1])
    sub_diag = jnp.concatenate([zero_row, -inner], axis=1)
    sup_diag = jnp.concatenate([-inner, zero_row], axis=1)
    solved = reduce_lines(sub_diag, main_diag, sup_diag, (tracer_part,), 1)[0]
    return lax.all_to_all(solved, "gy", split_axis=1, concat_axis=0, tiled=True)


def local(tracer, y_speed, z_speed, kappa):
    depth_z, depth_y, band = tracer.shape
    z_index = lax.axis_index("gz")
    z_count = lax.axis_size("gz")
    fields = jnp.stack([y_speed, z_speed, kappa])
    width = 1
    padded = padded_2(fields, (("gz", 1), ("gy", 2)), 1)
    state = tracer
    for step in range(NSUB):
        rimmed = padded_2(state, (("gz", 0), ("gy", 1)), 1)
        state = advect_once(rimmed, padded[0], padded[1])
    kappa_below = padded[2, width - 1 : width, width : width + depth_y]
    kappa_above = padded[2, width + depth_z : width + depth_z + 1, width : width + depth_y]
    lines = solve_rows(
        (
            lax.all_to_all(state, "gy", split_axis=0, concat_axis=1, tiled=True),
            lax.all_to_all(kappa, "gy", split_axis=0, concat_axis=1, tiled=True),
        )
    )
    inner = rate_const * 0.5 * (kappa[1:] + kappa[:-1])
    low_edge = jnp.where(
        z_index == 0, rate_const * kappa[:1], rate_const * 0.5 * (kappa[:1] + kappa_below)
    )
    high_edge = jnp.where(
        z_index == z_count - 1,
        rate_const * kappa[depth_z - 1 :],
        rate_const * 0.5 * (kappa[depth_z - 1 :] + kappa_above),
    )
    lower = jnp.concatenate([low_edge, inner], axis=0)
    upper = jnp.concatenate([inner, high_edge], axis=0)
    main_diag = 1.0 + lower + upper
    inner_count = depth_z - 1
    zero_row = jnp.zeros_like(kappa[:1])
    sub_local = jnp.concatenate([zero_row, -lower[1:inner_count]], axis=0)
    sup_local = jnp.concatenate([-upper[: inner_count - 1], zero_row], axis=0)
    zero_rows = jnp.zeros_like(kappa[: inner_count - 1])
    first_right = jnp.concatenate([lower[:1], zero_rows], axis=0)
    last_right = jnp.concatenate([zero_rows, upper[inner_count - 1 : inner_count]], axis=0)
    base, toward_low, toward_high = reduce_lines(
        sub_local,
        main_diag[:inner_count],
        sup_local,
        (lines[:inner_count], first_right, last_right),
        0,
    )
    following = from_behind(jnp.stack([base[0], toward_low[0], toward_high[0]]), "gz", -1)
    sep_low = lower[depth_z - 1]
    sep_high = upper[depth_z - 1]
    sub_red = jnp.where(z_index == 0, 0.0, -sep_low * toward_low[inner_count - 1])
    diag_red = (
        main_diag[depth_z - 1] - sep_low * toward_high[inner_count - 1] - sep_high * following[1]
    )
    sup_red = -sep_high * following[2]
    rhs_red = lines[depth_z - 1] + sep_low * base[inner_count - 1] + sep_high * following[0]
    equations = jnp.stack([sub_red, diag_red, sup_red, rhs_red])
    collected = lax.all_gather(equations[None], "gz", axis=0, tiled=True)
    values = reduce_lines(collected[:, 0], collected[:, 1], collected[:, 2], (collected[:, 3],), 0)[
        0
    ]
    sep_here = lax.dynamic_index_in_dim(values, z_index, axis=0, keepdims=False)
    previous = lax.dynamic_index_in_dim(values, jnp.maximum(z_index - 1, 0), axis=0, keepdims=False)
    sep_prev = jnp.where(z_index > 0, previous, 0.0)
    interior = base + sep_prev[None] * toward_low + sep_here[None] * toward_high
    return jnp.concatenate([interior, sep_here[None]], axis=0)


def solution(mesh):
    return jax.shard_map(
        local,
        mesh=mesh,
        in_specs=(
            P("gz", "gy", None),
            P("gz", "gy", None),
            P("gz", "gy", None),
            P("gz", "gy", None),
        ),
        out_specs=P("gz", "gy", None),
        check_vma=False,
    )
```

profile of v0, /device:TPU:2, one launch (start us, length us, event | category | flops | bytes accessed | tf_op | source)
XLA Modules:
  0.0 254.8 jit_solution(3350201011597019658)
XLA Ops:
  6.5 0.9 fusion.100
  7.4 3.8 %collective-permute-start.4 = (f32[1,32,128]{2,1,0:T(8,128)S(1)}, f32[1,32,128]{2,1,0:T(8,128)S(1)}, u32[]{:S(2)}, u32[]{:S(2)}) collective-permute-start(f32[1,32,128]{2,1,0:T(8,128)S(1)} %get-tuple-element.204), channel_id=1, source_target_pairs={{0,32},{32,64},{64,96},{96,128},{128,160},{160,192},{192,224},{224... | collective-permute-start | bytes 49160 | tf_op jit(solution)/shard_map/ppermute | solution.py:17
  12.0 3.8 %collective-permute-start = (f32[3,1,32,128]{3,2,1,0:T(8,128)S(1)}, f32[3,1,32,128]{3,2,1,0:T(8,128)S(1)}, u32[]{:S(2)}, u32[]{:S(2)}) collective-permute-start(f32[3,1,32,128]{3,2,1,0:T(8,128)S(1)} %get-tuple-element.65), channel_id=1, source_target_pairs={{0,32},{32,64},{64,96},{96,128},{128,160},{160,192},{192,224},{224... | collective-permute-start | bytes 147464 | tf_op jit(solution)/shard_map/ppermute | solution.py:17
  15.9 1.3 collective-permute-start.1
  17.2 1.3 collective-permute-start.5
  18.5 4.9 %collective-permute-done.5 = f32[1,32,128]{2,1,0:T(8,128)S(1)} collective-permute-done((f32[1,32,128]{2,1,0:T(8,128)S(1)}, f32[1,32,128]{2,1,0:T(8,128)S(1)}, u32[]{:S(2)}, u32[]{:S(2)}) %collective-permute-start.5) | collective-permute-done | bytes 16416 | tf_op jit(solution)/shard_map/ppermute | solution.py:18
  23.5 1.9 collective-permute-start.6
  25.4 5.8 %collective-permute-start.7 = (f32[34,1,128]{2,1,0:T(1,128)S(1)}, f32[34,1,128]{2,1,0:T(1,128)S(1)}, u32[]{:S(2)}, u32[]{:S(2)}) collective-permute-start(f32[34,1,128]{2,1,0:T(1,128)S(1)} %get-tuple-element.114), channel_id=1, source_target_pairs={{1,0},{2,1},{3,2},{4,3},{5,4},{6,5},{7,6},{8,7},{9,8},{10,9},{11,1... | collective-permute-start | bytes 52232 | tf_op jit(solution)/shard_map/ppermute | solution.py:18
  31.2 1.1 pad_maximum_fusion.11
  32.2 1.9 collective-permute-start.2
  34.2 5.8 %collective-permute-start.3 = (f32[3,34,1,128]{3,2,1,0:T(1,128)S(1)}, f32[3,34,1,128]{3,2,1,0:T(1,128)S(1)}, u32[]{:S(2)}, u32[]{:S(2)}) collective-permute-start(f32[3,34,1,128]{3,2,1,0:T(1,128)S(1)} %get-tuple-element.62), channel_id=1, source_target_pairs={{1,0},{2,1},{3,2},{4,3},{5,4},{6,5},{7,6},{8,7},{9,8},{10,9},{11,1... | collective-permute-start | bytes 156680 | tf_op jit(solution)/shard_map/ppermute | solution.py:18
  40.1 1.6 collective-permute-done.3
  41.7 1.4 pad_maximum_fusion
  44.1 4.9 %collective-permute-start.8 = (f32[1,32,128]{2,1,0:T(8,128)S(1)}, f32[1,32,128]{2,1,0:T(8,128)S(1)}, u32[]{:S(2)}, u32[]{:S(2)}) collective-permute-start(f32[1,32,128]{2,1,0:T(8,128)S(1)} %get-tuple-element.201), channel_id=1, source_target_pairs={{0,32},{32,64},{64,96},{96,128},{128,160},{160,192},{192,224},{224... | collective-permute-start | bytes 49160 | tf_op jit(solution)/shard_map/ppermute | solution.py:17
  49.1 1.3 collective-permute-start.9
  50.4 7.8 %all-to-all-start.1 = ((f32[32,32,128]{2,1,0:T(8,128)}), f32[32,32,128]{2,1,0:T(8,128)S(1)}, u32[]{:S(2)}, u32[]{:S(2)}) async-start(f32[32,32,128]{2,1,0:T(8,128)} %param.7), calls=%async_computation.1 | async-start | bytes 1048576 | tf_op jit(solution)/shard_map/all_to_all | solution.py:109
  58.2 2.0 collective-permute-start.10
  60.3 5.6 %collective-permute-start.11 = (f32[34,1,128]{2,1,0:T(1,128)S(1)}, f32[34,1,128]{2,1,0:T(1,128)S(1)}, u32[]{:S(2)}, u32[]{:S(2)}) collective-permute-start(f32[34,1,128]{2,1,0:T(1,128)S(1)} %get-tuple-element.112), channel_id=1, source_target_pairs={{1,0},{2,1},{3,2},{4,3},{5,4},{6,5},{7,6},{8,7},{9,8},{10,9},{11,1... | collective-permute-start | bytes 52232 | tf_op jit(solution)/shard_map/ppermute | solution.py:18
  65.9 1.3 add_multiply_fusion
  68.6 4.6 %collective-permute-start.12 = (f32[1,32,128]{2,1,0:T(8,128)S(1)}, f32[1,32,128]{2,1,0:T(8,128)S(1)}, u32[]{:S(2)}, u32[]{:S(2)}) collective-permute-start(f32[1,32,128]{2,1,0:T(8,128)S(1)} %get-tuple-element.199), channel_id=1, source_target_pairs={{0,32},{32,64},{64,96},{96,128},{128,160},{160,192},{192,224},{224... | collective-permute-start | bytes 49160 | tf_op jit(solution)/shard_map/ppermute | solution.py:17
  73.1 1.3 collective-permute-start.13
  74.5 5.4 %collective-permute-done.13 = f32[1,32,128]{2,1,0:T(8,128)S(1)} collective-permute-done((f32[1,32,128]{2,1,0:T(8,128)S(1)}, f32[1,32,128]{2,1,0:T(8,128)S(1)}, u32[]{:S(2)}, u32[]{:S(2)}) %collective-permute-start.13) | collective-permute-done | bytes 16416 | tf_op jit(solution)/shard_map/ppermute | solution.py:18
  80.0 1.9 collective-permute-start.14
  81.9 5.8 %collective-permute-start.15 = (f32[34,1,128]{2,1,0:T(1,128)S(1)}, f32[34,1,128]{2,1,0:T(1,128)S(1)}, u32[]{:S(2)}, u32[]{:S(2)}) collective-permute-start(f32[34,1,128]{2,1,0:T(1,128)S(1)} %get-tuple-element.110), channel_id=1, source_target_pairs={{1,0},{2,1},{3,2},{4,3},{5,4},{6,5},{7,6},{8,7},{9,8},{10,9},{11,1... | collective-permute-start | bytes 52232 | tf_op jit(solution)/shard_map/ppermute | solution.py:18
  87.7 1.1 pad_slice_fusion.2
  90.0 3.9 %collective-permute-start.16 = (f32[1,32,128]{2,1,0:T(8,128)S(1)}, f32[1,32,128]{2,1,0:T(8,128)S(1)}, u32[]{:S(2)}, u32[]{:S(2)}) collective-permute-start(f32[1,32,128]{2,1,0:T(8,128)S(1)} %get-tuple-element.197), channel_id=1, source_target_pairs={{0,32},{32,64},{64,96},{96,128},{128,160},{160,192},{192,224},{224... | collective-permute-start | bytes 49160 | tf_op jit(solution)/shard_map/ppermute | solution.py:17
  93.9 1.3 collective-permute-start.17
  95.2 0.8 pad_slice_fusion
  96.1 4.3 %collective-permute-done.17 = f32[1,32,128]{2,1,0:T(8,128)S(1)} collective-permute-done((f32[1,32,128]{2,1,0:T(8,128)S(1)}, f32[1,32,128]{2,1,0:T(8,128)S(1)}, u32[]{:S(2)}, u32[]{:S(2)}) %collective-permute-start.17) | collective-permute-done | bytes 16416 | tf_op jit(solution)/shard_map/ppermute | solution.py:18
  100.4 1.9 collective-permute-start.18
  102.4 5.8 %collective-permute-start.19 = (f32[34,1,128]{2,1,0:T(1,128)S(1)}, f32[34,1,128]{2,1,0:T(1,128)S(1)}, u32[]{:S(2)}, u32[]{:S(2)}) collective-permute-start(f32[34,1,128]{2,1,0:T(1,128)S(1)} %get-tuple-element.108), channel_id=1, source_target_pairs={{1,0},{2,1},{3,2},{4,3},{5,4},{6,5},{7,6},{8,7},{9,8},{10,9},{11,1... | collective-permute-start | bytes 52232 | tf_op jit(solution)/shard_map/ppermute | solution.py:18
  110.2 1.1 fusion.11
  111.3 8.0 %all-to-all-start = ((f32[32,32,128]{2,1,0:T(8,128)}), f32[32,32,128]{2,1,0:T(8,128)S(1)}, u32[]{:S(2)}, u32[]{:S(2)}) async-start(f32[32,32,128]{2,1,0:T(8,128)} %fusion.11), calls=%async_computation | async-start | bytes 1048576 | tf_op jit(solution)/shard_map/all_to_all | solution.py:108
  119.5 1.1 pad_slice_fusion.5
  120.7 8.5 %all-to-all-done = f32[32,32,128]{2,1,0:T(8,128)S(1)} async-done(((f32[32,32,128]{2,1,0:T(8,128)}), f32[32,32,128]{2,1,0:T(8,128)S(1)}, u32[]{:S(2)}, u32[]{:S(2)}) %all-to-all-start) | async-done | bytes 524320 | tf_op jit(solution)/shard_map/all_to_all | solution.py:108
  129.8 0.9 copy-done.8
  138.4 1.0 add_divide_fusion
  139.4 5.4 %all-to-all-start.2 = ((f32[1,1024,128]{2,0,1:T(1,128)}), f32[1,1024,128]{2,0,1:T(1,128)S(1)}, u32[]{:S(2)}, u32[]{:S(2)}) async-start(f32[1,1024,128]{2,0,1:T(1,128)} %bitcast.8), calls=%async_computation.2 | async-start | bytes 1048576 | tf_op jit(solution)/shard_map/all_to_all | solution.py:90
  145.2 0.9 fusion.60
  146.1 8.5 %all-to-all-done.2 = f32[1,1024,128]{2,0,1:T(1,128)S(1)} async-done(((f32[1,1024,128]{2,0,1:T(1,128)}), f32[1,1024,128]{2,0,1:T(1,128)S(1)}, u32[]{:S(2)}, u32[]{:S(2)}) %all-to-all-start.2) | async-done | bytes 524320 | tf_op jit(solution)/shard_map/all_to_all | solution.py:90
  154.7 0.9 copy-done.13
  159.2 0.9 multiply_add_fusion.29
  161.0 0.8 multiply_add_fusion.27
  164.1 1.3 collective-permute-start.20
  165.4 6.4 %collective-permute-done.20 = f32[3,32,128]{2,1,0:T(8,128)S(1)} collective-permute-done((f32[3,32,128]{2,1,0:T(8,128)S(1)}, f32[3,32,128]{2,1,0:T(8,128)S(1)}, u32[]{:S(2)}, u32[]{:S(2)}) %collective-permute-start.20) | collective-permute-done | bytes 49184 | tf_op jit(solution)/shard_map/ppermute | solution.py:26
  172.5 69.8 %all-gather.3.cloned.1.call-done = f32[64,32,128]{2,1,0:T(8,128)} async-done(((f32[4,32,128]{2,1,0:T(8,128)}), f32[64,32,128]{2,1,0:T(8,128)}) %all-gather.3.cloned.1.call-update) | async-done | bytes 1048592 | tf_op jit(solution)/shard_map/all_gather | solution.py:148
  242.3 1.9 slice_bitcast_fusion.11
  247.2 0.8 pad_maximum_fusion.5
  (203 shorter events, 25.5 us)
Async XLA Ops:
  6.5 11.9 %copy-start.5 = (f32[32,32,128]{2,1,0:T(8,128)S(1)}, f32[32,32,128]{2,1,0:T(8,128)}, u32[]{:S(2)}) copy-start(f32[32,32,128]{2,1,0:T(8,128)} %param.4) | copy-start | bytes 1572868
  6.5 24.6 %copy-start.2 = (f32[32,32,128]{2,1,0:T(8,128)S(1)}, f32[32,32,128]{2,1,0:T(8,128)}, u32[]{:S(2)}) copy-start(f32[32,32,128]{2,1,0:T(8,128)} %param.5) | copy-start | bytes 1572868
  6.5 24.6 %copy-start.1 = (f32[32,32,128]{2,1,0:T(8,128)S(1)}, f32[32,32,128]{2,1,0:T(8,128)}, u32[]{:S(2)}) copy-start(f32[32,32,128]{2,1,0:T(8,128)} %param.6) | copy-start | bytes 1572868
  7.4 11.1 %collective-permute-start.4 = (f32[1,32,128]{2,1,0:T(8,128)S(1)}, f32[1,32,128]{2,1,0:T(8,128)S(1)}, u32[]{:S(2)}, u32[]{:S(2)}) collective-permute-start(f32[1,32,128]{2,1,0:T(8,128)S(1)} %get-tuple-element.204), channel_id=1, source_target_pairs={{0,32},{32,64},{64,96},{96,128},{128,160},{160,192},{192,224},{224... | collective-permute-start | bytes 49160 | tf_op jit(solution)/shard_map/ppermute | solution.py:17
  12.0 19.1 %collective-permute-start = (f32[3,1,32,128]{3,2,1,0:T(8,128)S(1)}, f32[3,1,32,128]{3,2,1,0:T(8,128)S(1)}, u32[]{:S(2)}, u32[]{:S(2)}) collective-permute-start(f32[3,1,32,128]{3,2,1,0:T(8,128)S(1)} %get-tuple-element.65), channel_id=1, source_target_pairs={{0,32},{32,64},{64,96},{96,128},{128,160},{160,192},{192,224},{224... | collective-permute-start | bytes 147464 | tf_op jit(solution)/shard_map/ppermute | solution.py:17
  15.9 15.3 %collective-permute-start.1 = (f32[3,1,32,128]{3,2,1,0:T(8,128)S(1)}, f32[3,1,32,128]{3,2,1,0:T(8,128)S(1)}, u32[]{:S(2)}, u32[]{:S(2)}) collective-permute-start(f32[3,1,32,128]{3,2,1,0:T(8,128)S(1)} %get-tuple-element.66), channel_id=1, source_target_pairs={{32,0},{64,32},{96,64},{128,96},{160,128},{192,160},{224,192},{256... | collective-permute-start | bytes 147464 | tf_op jit(solution)/shard_map/ppermute | solution.py:18
  17.2 6.3 %collective-permute-start.5 = (f32[1,32,128]{2,1,0:T(8,128)S(1)}, f32[1,32,128]{2,1,0:T(8,128)S(1)}, u32[]{:S(2)}, u32[]{:S(2)}) collective-permute-start(f32[1,32,128]{2,1,0:T(8,128)S(1)} %get-tuple-element.203), channel_id=1, source_target_pairs={{32,0},{64,32},{96,64},{128,96},{160,128},{192,160},{224,192},{256... | collective-permute-start | bytes 49160 | tf_op jit(solution)/shard_map/ppermute | solution.py:18
  23.5 16.5 %collective-permute-start.6 = (f32[34,1,128]{2,1,0:T(1,128)S(1)}, f32[34,1,128]{2,1,0:T(1,128)S(1)}, u32[]{:S(2)}, u32[]{:S(2)}) collective-permute-start(f32[34,1,128]{2,1,0:T(1,128)S(1)} %get-tuple-element.113), channel_id=1, source_target_pairs={{0,1},{1,2},{2,3},{3,4},{4,5},{5,6},{6,7},{7,8},{8,9},{9,10},{10,1... | collective-permute-start | bytes 52232 | tf_op jit(solution)/shard_map/ppermute | solution.py:17
  25.4 14.6 %collective-permute-start.7 = (f32[34,1,128]{2,1,0:T(1,128)S(1)}, f32[34,1,128]{2,1,0:T(1,128)S(1)}, u32[]{:S(2)}, u32[]{:S(2)}) collective-permute-start(f32[34,1,128]{2,1,0:T(1,128)S(1)} %get-tuple-element.114), channel_id=1, source_target_pairs={{1,0},{2,1},{3,2},{4,3},{5,4},{6,5},{7,6},{8,7},{9,8},{10,9},{11,1... | collective-permute-start | bytes 52232 | tf_op jit(solution)/shard_map/ppermute | solution.py:18
  32.2 7.8 %collective-permute-start.2 = (f32[3,34,1,128]{3,2,1,0:T(1,128)S(1)}, f32[3,34,1,128]{3,2,1,0:T(1,128)S(1)}, u32[]{:S(2)}, u32[]{:S(2)}) collective-permute-start(f32[3,34,1,128]{3,2,1,0:T(1,128)S(1)} %get-tuple-element.61), channel_id=1, source_target_pairs={{0,1},{1,2},{2,3},{3,4},{4,5},{5,6},{6,7},{7,8},{8,9},{9,10},{10,1... | collective-permute-start | bytes 156680 | tf_op jit(solution)/shard_map/ppermute | solution.py:17
  34.2 7.5 %collective-permute-start.3 = (f32[3,34,1,128]{3,2,1,0:T(1,128)S(1)}, f32[3,34,1,128]{3,2,1,0:T(1,128)S(1)}, u32[]{:S(2)}, u32[]{:S(2)}) collective-permute-start(f32[3,34,1,128]{3,2,1,0:T(1,128)S(1)} %get-tuple-element.62), channel_id=1, source_target_pairs={{1,0},{2,1},{3,2},{4,3},{5,4},{6,5},{7,6},{8,7},{9,8},{10,9},{11,1... | collective-permute-start | bytes 156680 | tf_op jit(solution)/shard_map/ppermute | solution.py:18
  44.1 14.0 %collective-permute-start.8 = (f32[1,32,128]{2,1,0:T(8,128)S(1)}, f32[1,32,128]{2,1,0:T(8,128)S(1)}, u32[]{:S(2)}, u32[]{:S(2)}) collective-permute-start(f32[1,32,128]{2,1,0:T(8,128)S(1)} %get-tuple-element.201), channel_id=1, source_target_pairs={{0,32},{32,64},{64,96},{96,128},{128,160},{160,192},{192,224},{224... | collective-permute-start | bytes 49160 | tf_op jit(solution)/shard_map/ppermute | solution.py:17
  49.1 9.1 %collective-permute-start.9 = (f32[1,32,128]{2,1,0:T(8,128)S(1)}, f32[1,32,128]{2,1,0:T(8,128)S(1)}, u32[]{:S(2)}, u32[]{:S(2)}) collective-permute-start(f32[1,32,128]{2,1,0:T(8,128)S(1)} %get-tuple-element.202), channel_id=1, source_target_pairs={{32,0},{64,32},{96,64},{128,96},{160,128},{192,160},{224,192},{256... | collective-permute-start | bytes 49160 | tf_op jit(solution)/shard_map/ppermute | solution.py:18
  50.4 60.9 %all-to-all-start.1 = ((f32[32,32,128]{2,1,0:T(8,128)}), f32[32,32,128]{2,1,0:T(8,128)S(1)}, u32[]{:S(2)}, u32[]{:S(2)}) async-start(f32[32,32,128]{2,1,0:T(8,128)} %param.7), calls=%async_computation.1 | async-start | bytes 1048576 | tf_op jit(solution)/shard_map/all_to_all | solution.py:109
  58.2 9.4 %collective-permute-start.10 = (f32[34,1,128]{2,1,0:T(1,128)S(1)}, f32[34,1,128]{2,1,0:T(1,128)S(1)}, u32[]{:S(2)}, u32[]{:S(2)}) collective-permute-start(f32[34,1,128]{2,1,0:T(1,128)S(1)} %get-tuple-element.111), channel_id=1, source_target_pairs={{0,1},{1,2},{2,3},{3,4},{4,5},{5,6},{6,7},{7,8},{8,9},{9,10},{10,1... | collective-permute-start | bytes 52232 | tf_op jit(solution)/shard_map/ppermute | solution.py:17
  60.3 7.4 %collective-permute-start.11 = (f32[34,1,128]{2,1,0:T(1,128)S(1)}, f32[34,1,128]{2,1,0:T(1,128)S(1)}, u32[]{:S(2)}, u32[]{:S(2)}) collective-permute-start(f32[34,1,128]{2,1,0:T(1,128)S(1)} %get-tuple-element.112), channel_id=1, source_target_pairs={{1,0},{2,1},{3,2},{4,3},{5,4},{6,5},{7,6},{8,7},{9,8},{10,9},{11,1... | collective-permute-start | bytes 52232 | tf_op jit(solution)/shard_map/ppermute | solution.py:18
  67.2 21.6 %copy-start.3 = (f32[31,32,128]{2,1,0:T(8,128)}, f32[31,32,128]{2,1,0:T(8,128)S(1)}, u32[]{:S(2)}) copy-start(f32[31,32,128]{2,1,0:T(8,128)S(1)} %add_multiply_fusion) | copy-start | bytes 1523716
  68.6 6.0 %collective-permute-start.12 = (f32[1,32,128]{2,1,0:T(8,128)S(1)}, f32[1,32,128]{2,1,0:T(8,128)S(1)}, u32[]{:S(2)}, u32[]{:S(2)}) collective-permute-start(f32[1,32,128]{2,1,0:T(8,128)S(1)} %get-tuple-element.199), channel_id=1, source_target_pairs={{0,32},{32,64},{64,96},{96,128},{128,160},{160,192},{192,224},{224... | collective-permute-start | bytes 49160 | tf_op jit(solution)/shard_map/ppermute | solution.py:17
  73.1 6.8 %collective-permute-start.13 = (f32[1,32,128]{2,1,0:T(8,128)S(1)}, f32[1,32,128]{2,1,0:T(8,128)S(1)}, u32[]{:S(2)}, u32[]{:S(2)}) collective-permute-start(f32[1,32,128]{2,1,0:T(8,128)S(1)} %get-tuple-element.200), channel_id=1, source_target_pairs={{32,0},{64,32},{96,64},{128,96},{160,128},{192,160},{224,192},{256... | collective-permute-start | bytes 49160 | tf_op jit(solution)/shard_map/ppermute | solution.py:18
  80.0 8.8 %collective-permute-start.14 = (f32[34,1,128]{2,1,0:T(1,128)S(1)}, f32[34,1,128]{2,1,0:T(1,128)S(1)}, u32[]{:S(2)}, u32[]{:S(2)}) collective-permute-start(f32[34,1,128]{2,1,0:T(1,128)S(1)} %get-tuple-element.109), channel_id=1, source_target_pairs={{0,1},{1,2},{2,3},{3,4},{4,5},{5,6},{6,7},{7,8},{8,9},{9,10},{10,1... | collective-permute-start | bytes 52232 | tf_op jit(solution)/shard_map/ppermute | solution.py:17
  81.9 7.2 %collective-permute-start.15 = (f32[34,1,128]{2,1,0:T(1,128)S(1)}, f32[34,1,128]{2,1,0:T(1,128)S(1)}, u32[]{:S(2)}, u32[]{:S(2)}) collective-permute-start(f32[34,1,128]{2,1,0:T(1,128)S(1)} %get-tuple-element.110), channel_id=1, source_target_pairs={{1,0},{2,1},{3,2},{4,3},{5,4},{6,5},{7,6},{8,7},{9,8},{10,9},{11,1... | collective-permute-start | bytes 52232 | tf_op jit(solution)/shard_map/ppermute | solution.py:18
  90.0 6.1 %collective-permute-start.16 = (f32[1,32,128]{2,1,0:T(8,128)S(1)}, f32[1,32,128]{2,1,0:T(8,128)S(1)}, u32[]{:S(2)}, u32[]{:S(2)}) collective-permute-start(f32[1,32,128]{2,1,0:T(8,128)S(1)} %get-tuple-element.197), channel_id=1, source_target_pairs={{0,32},{32,64},{64,96},{96,128},{128,160},{160,192},{192,224},{224... | collective-permute-start | bytes 49160 | tf_op jit(solution)/shard_map/ppermute | solution.py:17
  93.9 6.5 %collective-permute-start.17 = (f32[1,32,128]{2,1,0:T(8,128)S(1)}, f32[1,32,128]{2,1,0:T(8,128)S(1)}, u32[]{:S(2)}, u32[]{:S(2)}) collective-permute-start(f32[1,32,128]{2,1,0:T(8,128)S(1)} %get-tuple-element.198), channel_id=1, source_target_pairs={{32,0},{64,32},{96,64},{128,96},{160,128},{192,160},{224,192},{256... | collective-permute-start | bytes 49160 | tf_op jit(solution)/shard_map/ppermute | solution.py:18
  100.4 8.4 %collective-permute-start.18 = (f32[34,1,128]{2,1,0:T(1,128)S(1)}, f32[34,1,128]{2,1,0:T(1,128)S(1)}, u32[]{:S(2)}, u32[]{:S(2)}) collective-permute-start(f32[34,1,128]{2,1,0:T(1,128)S(1)} %get-tuple-element.107), channel_id=1, source_target_pairs={{0,1},{1,2},{2,3},{3,4},{4,5},{5,6},{6,7},{7,8},{8,9},{9,10},{10,1... | collective-permute-start | bytes 52232 | tf_op jit(solution)/shard_map/ppermute | solution.py:17
  102.4 7.2 %collective-permute-start.19 = (f32[34,1,128]{2,1,0:T(1,128)S(1)}, f32[34,1,128]{2,1,0:T(1,128)S(1)}, u32[]{:S(2)}, u32[]{:S(2)}) collective-permute-start(f32[34,1,128]{2,1,0:T(1,128)S(1)} %get-tuple-element.108), channel_id=1, source_target_pairs={{1,0},{2,1},{3,2},{4,3},{5,4},{6,5},{7,6},{8,7},{9,8},{10,9},{11,1... | collective-permute-start | bytes 52232 | tf_op jit(solution)/shard_map/ppermute | solution.py:18
  111.3 17.8 %all-to-all-start = ((f32[32,32,128]{2,1,0:T(8,128)}), f32[32,32,128]{2,1,0:T(8,128)S(1)}, u32[]{:S(2)}, u32[]{:S(2)}) async-start(f32[32,32,128]{2,1,0:T(8,128)} %fusion.11), calls=%async_computation | async-start | bytes 1048576 | tf_op jit(solution)/shard_map/all_to_all | solution.py:108
  129.6 1.0 copy-start.8
  129.6 1.2 copy-start.9
  138.3 6.8 %copy-start.4 = (f32[31,32,128]{2,1,0:T(8,128)S(1)}, f32[31,32,128]{2,1,0:T(8,128)}, u32[]{:S(2)}) copy-start(f32[31,32,128]{2,1,0:T(8,128)} %copy-done.3) | copy-start | bytes 1523716
  139.4 15.2 %all-to-all-start.2 = ((f32[1,1024,128]{2,0,1:T(1,128)}), f32[1,1024,128]{2,0,1:T(1,128)S(1)}, u32[]{:S(2)}, u32[]{:S(2)}) async-start(f32[1,1024,128]{2,0,1:T(1,128)} %bitcast.8), calls=%async_computation.2 | async-start | bytes 1048576 | tf_op jit(solution)/shard_map/all_to_all | solution.py:90
  144.8 97.5 %all-gather.3.cloned.1.call-start = ((), (), s32[]{:S(2)}) async-start(), calls=%async_computation.3 | async-start | bytes 1114112 | tf_op jit(solution)/shard_map/all_gather | solution.py:148
  154.6 1.0 copy-start.13
  156.2 1.0 copy-start.10
  156.2 1.2 copy-start.11
  156.3 1.3 copy-start.12
  163.6 8.2 %copy-start.6 = (f32[31,32,128]{2,1,0:T(8,128)}, f32[31,32,128]{2,1,0:T(8,128)S(1)}, u32[]{:S(2)}) copy-start(f32[31,32,128]{2,1,0:T(8,128)S(1)} %get-tuple-element.60) | copy-start | bytes 1523716
  164.1 7.7 %collective-permute-start.20 = (f32[3,32,128]{2,1,0:T(8,128)S(1)}, f32[3,32,128]{2,1,0:T(8,128)S(1)}, u32[]{:S(2)}, u32[]{:S(2)}) collective-permute-start(f32[3,32,128]{2,1,0:T(8,128)S(1)} %pad_maximum_fusion.15), channel_id=1, source_target_pairs={{32,0},{64,32},{96,64},{128,96},{160,128},{192,160},{224,192},{256... | collective-permute-start | bytes 147464 | tf_op jit(solution)/shard_map/ppermute | solution.py:26
  242.3 2.0 copy-start
  245.9 1.0 copy-start.7
Sparse Core Ops, SparseCore 0:
  172.6 69.6 all-gather.2
where the time goes:
time: 256 us; the launch traced here: 255 us
  waiting for transfers between devices  111 us (43%)
  starting transfers between devices  88.6 us (35%)
  other arithmetic  24.4 us (10%)
  local copies, waits for them, and re-layouts  16.1 us (6%)
  between operations  14.8 us (6%)
    all_gather x1, waiting for transfers between devices, local(): collected = lax.all_gather(equations[None], 'gz', axis=0, tiled=True)  69.8 us
    ppermute x10, starting transfers between devices, padded_2(): after = lax.ppermute(leading, axis, down)  35.1 us
    ppermute x10, starting transfers between devices, padded_2(): before = lax.ppermute(last, axis, up)  30.7 us
    ppermute x10, waiting for transfers between devices, padded_2(): after = lax.ppermute(leading, axis, down)  17.3 us
    all_to_all x1, waiting for transfers between devices, solve_rows(): return lax.all_to_all(solved, 'gy', split_axis=1, concat_axis=0, tiled=True)  8.48 us
    all_to_all x1, waiting for transfers between devices, local(): lax.all_to_all(state, 'gy', split_axis=0, concat_axis=1, tiled=True)  8.45 us
    all_to_all x1, starting transfers between devices, local(): lax.all_to_all(state, 'gy', split_axis=0, concat_axis=1, tiled=True)  8.02 us
    all_to_all x1, starting transfers between devices, local(): lax.all_to_all(kappa, 'gy', split_axis=0, concat_axis=1, tiled=True)  7.77 us
  transfers between devices with their start and end apart: 25, of which 12 were waited for; matrix products, arithmetic and copies ran while one was open for 5% of the time, Pallas kernels for 0%

commit v1 on v0

--- a/solution.py
+++ b/solution.py
@@ -145,7 +145,15 @@
     sup_red = -sep_high * following[2]
     rhs_red = lines[depth_z - 1] + sep_low * base[inner_count - 1] + sep_high * following[0]
     equations = jnp.stack([sub_red, diag_red, sup_red, rhs_red])
-    collected = lax.all_gather(equations[None], "gz", axis=0, tiled=True)
+
+    def unite_kinds(axis_name, in_dim, panel):
+        shaped = jnp.concatenate(
+            lax.all_to_all(jnp.stack(lax.axis_size(axis_name) * [panel], axis=0), axis_name, 0, 0),
+            in_dim,
+        )
+        return shaped
+
+    collected = unite_kinds("gz", 0, equations[None])
     values = reduce_lines(collected[:, 0], collected[:, 1], collected[:, 2], (collected[:, 3],), 0)[
         0
     ]

time: 256 us -> 235 us (0.918)
  the two profiles are of different devices: /device:TPU:2 before, /device:TPU:32 now
where the time goes in v1:
time: 235 us; the launch traced here: 233 us
  starting transfers between devices  100 us (43%)
  waiting for transfers between devices  92.3 us (39%)
  other arithmetic  23.8 us (10%)
  local copies, waits for them, and re-layouts  15.5 us (7%)
    all_to_all x1, waiting for transfers between devices, unite_kinds(): lax.all_to_all(jnp.stack(lax.axis_size(axis_name) * [panel], axis=0), axi...  49.5 us
    ppermute x10, starting transfers between devices, padded_2(): before = lax.ppermute(last, axis, up)  37.1 us
    ppermute x10, waiting for transfers between devices, padded_2(): after = lax.ppermute(leading, axis, down)  18.8 us
    ppermute x10, starting transfers between devices, padded_2(): after = lax.ppermute(leading, axis, down)  16.4 us
    all_to_all x1, starting transfers between devices, local(): lax.all_to_all(state, 'gy', split_axis=0, concat_axis=1, tiled=True)  15.4 us
    all_to_all x1, starting transfers between devices, local(): lax.all_to_all(kappa, 'gy', split_axis=0, concat_axis=1, tiled=True)  12.8 us
    all_to_all x1, starting transfers between devices, unite_kinds(): lax.all_to_all(jnp.stack(lax.axis_size(axis_name) * [panel], axis=0), axi...  12.3 us
    all_to_all x1, waiting for transfers between devices, solve_rows(): return lax.all_to_all(solved, 'gy', split_axis=1, concat_axis=0, tiled=True)  9.81 us
  transfers between devices with their start and end apart: 25, of which 11 were waited for; matrix products, arithmetic and copies ran while one was open for 5% of the time, Pallas kernels for 0%

profile of v1, /device:TPU:32, one launch (start us, length us, event | category | flops | bytes accessed | tf_op | source)
XLA Modules:
  0.0 233.3 jit_solution(10036989041179189057)
XLA Ops:
  0.0 0.9 fusion.98
  0.9 3.8 %collective-permute-start.4 = (f32[1,32,128]{2,1,0:T(8,128)S(1)}, f32[1,32,128]{2,1,0:T(8,128)S(1)}, u32[]{:S(2)}, u32[]{:S(2)}) collective-permute-start(f32[1,32,128]{2,1,0:T(8,128)S(1)} %get-tuple-element.204), channel_id=1, source_target_pairs={{0,32},{32,64},{64,96},{96,128},{128,160},{160,192},{192,224},{224... | collective-permute-start | bytes 49160 | tf_op jit(solution)/shard_map/ppermute | solution.py:17
  5.5 3.8 %collective-permute-start = (f32[3,1,32,128]{3,2,1,0:T(8,128)S(1)}, f32[3,1,32,128]{3,2,1,0:T(8,128)S(1)}, u32[]{:S(2)}, u32[]{:S(2)}) collective-permute-start(f32[3,1,32,128]{3,2,1,0:T(8,128)S(1)} %get-tuple-element.65), channel_id=1, source_target_pairs={{0,32},{32,64},{64,96},{96,128},{128,160},{160,192},{192,224},{224... | collective-permute-start | bytes 147464 | tf_op jit(solution)/shard_map/ppermute | solution.py:17
  9.3 2.3 collective-permute-start.1
  11.6 1.9 collective-permute-start.5
  13.6 4.4 %collective-permute-done.5 = f32[1,32,128]{2,1,0:T(8,128)S(1)} collective-permute-done((f32[1,32,128]{2,1,0:T(8,128)S(1)}, f32[1,32,128]{2,1,0:T(8,128)S(1)}, u32[]{:S(2)}, u32[]{:S(2)}) %collective-permute-start.5) | collective-permute-done | bytes 16416 | tf_op jit(solution)/shard_map/ppermute | solution.py:18
  18.0 1.3 collective-permute-start.6
  19.3 1.3 collective-permute-start.7
  20.7 1.1 pad_maximum_fusion.11
  21.7 4.8 %collective-permute-start.2 = (f32[3,34,1,128]{3,2,1,0:T(1,128)S(1)}, f32[3,34,1,128]{3,2,1,0:T(1,128)S(1)}, u32[]{:S(2)}, u32[]{:S(2)}) collective-permute-start(f32[3,34,1,128]{3,2,1,0:T(1,128)S(1)} %get-tuple-element.61), channel_id=1, source_target_pairs={{0,1},{1,2},{2,3},{3,4},{4,5},{5,6},{6,7},{7,8},{8,9},{9,10},{10,1... | collective-permute-start | bytes 156680 | tf_op jit(solution)/shard_map/ppermute | solution.py:17
  26.6 1.3 collective-permute-start.3
  28.0 2.9 %collective-permute-done.3 = f32[3,34,1,128]{3,2,1,0:T(1,128)S(1)} collective-permute-done((f32[3,34,1,128]{3,2,1,0:T(1,128)S(1)}, f32[3,34,1,128]{3,2,1,0:T(1,128)S(1)}, u32[]{:S(2)}, u32[]{:S(2)}) %collective-permute-start.3) | collective-permute-done | bytes 52256 | tf_op jit(solution)/shard_map/ppermute | solution.py:18
  31.0 1.4 pad_maximum_fusion
  33.4 3.9 %collective-permute-start.8 = (f32[1,32,128]{2,1,0:T(8,128)S(1)}, f32[1,32,128]{2,1,0:T(8,128)S(1)}, u32[]{:S(2)}, u32[]{:S(2)}) collective-permute-start(f32[1,32,128]{2,1,0:T(8,128)S(1)} %get-tuple-element.201), channel_id=1, source_target_pairs={{0,32},{32,64},{64,96},{96,128},{128,160},{160,192},{192,224},{224... | collective-permute-start | bytes 49160 | tf_op jit(solution)/shard_map/ppermute | solution.py:17
  37.3 1.9 collective-permute-start.9
  39.3 12.8 %all-to-all-start.1 = ((f32[32,32,128]{2,1,0:T(8,128)}), f32[32,32,128]{2,1,0:T(8,128)S(1)}, u32[]{:S(2)}, u32[]{:S(2)}) async-start(f32[32,32,128]{2,1,0:T(8,128)} %param.7), calls=%async_computation.1 | async-start | bytes 1048576 | tf_op jit(solution)/shard_map/all_to_all | solution.py:109
  52.1 2.2 collective-permute-start.10
  54.3 1.3 collective-permute-start.11
  55.6 1.3 add_multiply_fusion
  56.9 1.6 collective-permute-done.11
  59.4 5.1 %collective-permute-start.12 = (f32[1,32,128]{2,1,0:T(8,128)S(1)}, f32[1,32,128]{2,1,0:T(8,128)S(1)}, u32[]{:S(2)}, u32[]{:S(2)}) collective-permute-start(f32[1,32,128]{2,1,0:T(8,128)S(1)} %get-tuple-element.199), channel_id=1, source_target_pairs={{0,32},{32,64},{64,96},{96,128},{128,160},{160,192},{192,224},{224... | collective-permute-start | bytes 49160 | tf_op jit(solution)/shard_map/ppermute | solution.py:17
  64.6 1.9 collective-permute-start.13
  66.6 3.6 %collective-permute-done.13 = f32[1,32,128]{2,1,0:T(8,128)S(1)} collective-permute-done((f32[1,32,128]{2,1,0:T(8,128)S(1)}, f32[1,32,128]{2,1,0:T(8,128)S(1)}, u32[]{:S(2)}, u32[]{:S(2)}) %collective-permute-start.13) | collective-permute-done | bytes 16416 | tf_op jit(solution)/shard_map/ppermute | solution.py:18
  70.2 4.0 %collective-permute-start.14 = (f32[34,1,128]{2,1,0:T(1,128)S(1)}, f32[34,1,128]{2,1,0:T(1,128)S(1)}, u32[]{:S(2)}, u32[]{:S(2)}) collective-permute-start(f32[34,1,128]{2,1,0:T(1,128)S(1)} %get-tuple-element.109), channel_id=1, source_target_pairs={{0,1},{1,2},{2,3},{3,4},{4,5},{5,6},{6,7},{7,8},{8,9},{9,10},{10,1... | collective-permute-start | bytes 52232 | tf_op jit(solution)/shard_map/ppermute | solution.py:17
  74.3 1.3 collective-permute-start.15
  75.6 1.1 pad_slice_fusion.2
  78.3 4.9 %collective-permute-start.16 = (f32[1,32,128]{2,1,0:T(8,128)S(1)}, f32[1,32,128]{2,1,0:T(8,128)S(1)}, u32[]{:S(2)}, u32[]{:S(2)}) collective-permute-start(f32[1,32,128]{2,1,0:T(8,128)S(1)} %get-tuple-element.197), channel_id=1, source_target_pairs={{0,32},{32,64},{64,96},{96,128},{128,160},{160,192},{192,224},{224... | collective-permute-start | bytes 49160 | tf_op jit(solution)/shard_map/ppermute | solution.py:17
  83.1 1.9 collective-permute-start.17
  85.9 3.9 %collective-permute-done.17 = f32[1,32,128]{2,1,0:T(8,128)S(1)} collective-permute-done((f32[1,32,128]{2,1,0:T(8,128)S(1)}, f32[1,32,128]{2,1,0:T(8,128)S(1)}, u32[]{:S(2)}, u32[]{:S(2)}) %collective-permute-start.17) | collective-permute-done | bytes 16416 | tf_op jit(solution)/shard_map/ppermute | solution.py:18
  89.8 3.2 %collective-permute-start.18 = (f32[34,1,128]{2,1,0:T(1,128)S(1)}, f32[34,1,128]{2,1,0:T(1,128)S(1)}, u32[]{:S(2)}, u32[]{:S(2)}) collective-permute-start(f32[34,1,128]{2,1,0:T(1,128)S(1)} %get-tuple-element.107), channel_id=1, source_target_pairs={{0,1},{1,2},{2,3},{3,4},{4,5},{5,6},{6,7},{7,8},{8,9},{9,10},{10,1... | collective-permute-start | bytes 52232 | tf_op jit(solution)/shard_map/ppermute | solution.py:17
  93.0 1.3 collective-permute-start.19
  95.1 1.7 collective-permute-done.19
  97.4 1.1 fusion.11
  98.5 15.4 %all-to-all-start = ((f32[32,32,128]{2,1,0:T(8,128)}), f32[32,32,128]{2,1,0:T(8,128)S(1)}, u32[]{:S(2)}, u32[]{:S(2)}) async-start(f32[32,32,128]{2,1,0:T(8,128)} %fusion.11), calls=%async_computation | async-start | bytes 1048576 | tf_op jit(solution)/shard_map/all_to_all | solution.py:108
  114.2 1.1 pad_slice_fusion.5
  115.3 9.6 %all-to-all-done = f32[32,32,128]{2,1,0:T(8,128)S(1)} async-done(((f32[32,32,128]{2,1,0:T(8,128)}), f32[32,32,128]{2,1,0:T(8,128)S(1)}, u32[]{:S(2)}, u32[]{:S(2)}) %all-to-all-start) | async-done | bytes 524320 | tf_op jit(solution)/shard_map/all_to_all | solution.py:108
  125.6 0.9 copy-done.7
  134.1 1.0 add_divide_fusion
  135.2 4.4 %all-to-all-start.2 = ((f32[1,1024,128]{2,0,1:T(1,128)}), f32[1,1024,128]{2,0,1:T(1,128)S(1)}, u32[]{:S(2)}, u32[]{:S(2)}) async-start(f32[1,1024,128]{2,0,1:T(1,128)} %bitcast.8), calls=%async_computation.2 | async-start | bytes 1048576 | tf_op jit(solution)/shard_map/all_to_all | solution.py:90
  139.7 0.9 fusion.58
  140.6 9.8 %all-to-all-done.2 = f32[1,1024,128]{2,0,1:T(1,128)S(1)} async-done(((f32[1,1024,128]{2,0,1:T(1,128)}), f32[1,1024,128]{2,0,1:T(1,128)S(1)}, u32[]{:S(2)}, u32[]{:S(2)}) %all-to-all-start.2) | async-done | bytes 524320 | tf_op jit(solution)/shard_map/all_to_all | solution.py:90
  150.5 0.9 copy-done.12
  155.0 0.9 multiply_add_fusion.29
  159.9 1.9 collective-permute-start.20
  161.8 4.5 %collective-permute-done.20 = f32[3,32,128]{2,1,0:T(8,128)S(1)} collective-permute-done((f32[3,32,128]{2,1,0:T(8,128)S(1)}, f32[3,32,128]{2,1,0:T(8,128)S(1)}, u32[]{:S(2)}, u32[]{:S(2)}) %collective-permute-start.20) | collective-permute-done | bytes 49184 | tf_op jit(solution)/shard_map/ppermute | solution.py:26
  166.3 1.1 stack.31
  167.4 12.3 %all-to-all-start.3 = ((f32[16,1,4,32,128]{4,3,2,1,0:T(8,128)}), f32[16,1,4,32,128]{4,3,2,1,0:T(8,128)S(1)}, u32[]{:S(2)}, u32[]{:S(2)}) async-start(f32[16,1,4,32,128]{4,3,2,1,0:T(8,128)} %stack.31), calls=%async_computation.3 | async-start | bytes 2097152 | tf_op jit(solution)/shard_map/all_to_all | solution.py:151
  179.7 49.5 %all-to-all-done.3 = f32[16,1,4,32,128]{4,3,2,1,0:T(8,128)S(1)} async-done(((f32[16,1,4,32,128]{4,3,2,1,0:T(8,128)}), f32[16,1,4,32,128]{4,3,2,1,0:T(8,128)S(1)}, u32[]{:S(2)}, u32[]{:S(2)}) %all-to-all-start.3) | async-done | bytes 1048608 | tf_op jit(solution)/shard_map/all_to_all | solution.py:151
  (202 shorter events, 26.4 us)
Async XLA Ops:
  0.0 13.6 %copy-start.4 = (f32[32,32,128]{2,1,0:T(8,128)S(1)}, f32[32,32,128]{2,1,0:T(8,128)}, u32[]{:S(2)}) copy-start(f32[32,32,128]{2,1,0:T(8,128)} %param.4) | copy-start | bytes 1572868
  0.0 20.7 %copy-start.1 = (f32[32,32,128]{2,1,0:T(8,128)S(1)}, f32[32,32,128]{2,1,0:T(8,128)}, u32[]{:S(2)}) copy-start(f32[32,32,128]{2,1,0:T(8,128)} %param.5) | copy-start | bytes 1572868
  0.0 20.7 %copy-start = (f32[32,32,128]{2,1,0:T(8,128)S(1)}, f32[32,32,128]{2,1,0:T(8,128)}, u32[]{:S(2)}) copy-start(f32[32,32,128]{2,1,0:T(8,128)} %param.6) | copy-start | bytes 1572868
  0.9 12.7 %collective-permute-start.4 = (f32[1,32,128]{2,1,0:T(8,128)S(1)}, f32[1,32,128]{2,1,0:T(8,128)S(1)}, u32[]{:S(2)}, u32[]{:S(2)}) collective-permute-start(f32[1,32,128]{2,1,0:T(8,128)S(1)} %get-tuple-element.204), channel_id=1, source_target_pairs={{0,32},{32,64},{64,96},{96,128},{128,160},{160,192},{192,224},{224... | collective-permute-start | bytes 49160 | tf_op jit(solution)/shard_map/ppermute | solution.py:17
  5.5 15.1 %collective-permute-start = (f32[3,1,32,128]{3,2,1,0:T(8,128)S(1)}, f32[3,1,32,128]{3,2,1,0:T(8,128)S(1)}, u32[]{:S(2)}, u32[]{:S(2)}) collective-permute-start(f32[3,1,32,128]{3,2,1,0:T(8,128)S(1)} %get-tuple-element.65), channel_id=1, source_target_pairs={{0,32},{32,64},{64,96},{96,128},{128,160},{160,192},{192,224},{224... | collective-permute-start | bytes 147464 | tf_op jit(solution)/shard_map/ppermute | solution.py:17
  9.3 11.3 %collective-permute-start.1 = (f32[3,1,32,128]{3,2,1,0:T(8,128)S(1)}, f32[3,1,32,128]{3,2,1,0:T(8,128)S(1)}, u32[]{:S(2)}, u32[]{:S(2)}) collective-permute-start(f32[3,1,32,128]{3,2,1,0:T(8,128)S(1)} %get-tuple-element.66), channel_id=1, source_target_pairs={{32,0},{64,32},{96,64},{128,96},{160,128},{192,160},{224,192},{256... | collective-permute-start | bytes 147464 | tf_op jit(solution)/shard_map/ppermute | solution.py:18
  11.6 6.4 %collective-permute-start.5 = (f32[1,32,128]{2,1,0:T(8,128)S(1)}, f32[1,32,128]{2,1,0:T(8,128)S(1)}, u32[]{:S(2)}, u32[]{:S(2)}) collective-permute-start(f32[1,32,128]{2,1,0:T(8,128)S(1)} %get-tuple-element.203), channel_id=1, source_target_pairs={{32,0},{64,32},{96,64},{128,96},{160,128},{192,160},{224,192},{256... | collective-permute-start | bytes 49160 | tf_op jit(solution)/shard_map/ppermute | solution.py:18
  18.0 9.9 %collective-permute-start.6 = (f32[34,1,128]{2,1,0:T(1,128)S(1)}, f32[34,1,128]{2,1,0:T(1,128)S(1)}, u32[]{:S(2)}, u32[]{:S(2)}) collective-permute-start(f32[34,1,128]{2,1,0:T(1,128)S(1)} %get-tuple-element.113), channel_id=1, source_target_pairs={{0,1},{1,2},{2,3},{3,4},{4,5},{5,6},{6,7},{7,8},{8,9},{9,10},{10,1... | collective-permute-start | bytes 52232 | tf_op jit(solution)/shard_map/ppermute | solution.py:17
  19.3 8.6 %collective-permute-start.7 = (f32[34,1,128]{2,1,0:T(1,128)S(1)}, f32[34,1,128]{2,1,0:T(1,128)S(1)}, u32[]{:S(2)}, u32[]{:S(2)}) collective-permute-start(f32[34,1,128]{2,1,0:T(1,128)S(1)} %get-tuple-element.114), channel_id=1, source_target_pairs={{1,0},{2,1},{3,2},{4,3},{5,4},{6,5},{7,6},{8,7},{9,8},{10,9},{11,1... | collective-permute-start | bytes 52232 | tf_op jit(solution)/shard_map/ppermute | solution.py:18
  21.7 6.3 %collective-permute-start.2 = (f32[3,34,1,128]{3,2,1,0:T(1,128)S(1)}, f32[3,34,1,128]{3,2,1,0:T(1,128)S(1)}, u32[]{:S(2)}, u32[]{:S(2)}) collective-permute-start(f32[3,34,1,128]{3,2,1,0:T(1,128)S(1)} %get-tuple-element.61), channel_id=1, source_target_pairs={{0,1},{1,2},{2,3},{3,4},{4,5},{5,6},{6,7},{7,8},{8,9},{9,10},{10,1... | collective-permute-start | bytes 156680 | tf_op jit(solution)/shard_map/ppermute | solution.py:17
  26.6 4.4 %collective-permute-start.3 = (f32[3,34,1,128]{3,2,1,0:T(1,128)S(1)}, f32[3,34,1,128]{3,2,1,0:T(1,128)S(1)}, u32[]{:S(2)}, u32[]{:S(2)}) collective-permute-start(f32[3,34,1,128]{3,2,1,0:T(1,128)S(1)} %get-tuple-element.62), channel_id=1, source_target_pairs={{1,0},{2,1},{3,2},{4,3},{5,4},{6,5},{7,6},{8,7},{9,8},{10,9},{11,1... | collective-permute-start | bytes 156680 | tf_op jit(solution)/shard_map/ppermute | solution.py:18
  33.4 18.7 %collective-permute-start.8 = (f32[1,32,128]{2,1,0:T(8,128)S(1)}, f32[1,32,128]{2,1,0:T(8,128)S(1)}, u32[]{:S(2)}, u32[]{:S(2)}) collective-permute-start(f32[1,32,128]{2,1,0:T(8,128)S(1)} %get-tuple-element.201), channel_id=1, source_target_pairs={{0,32},{32,64},{64,96},{96,128},{128,160},{160,192},{192,224},{224... | collective-permute-start | bytes 49160 | tf_op jit(solution)/shard_map/ppermute | solution.py:17
  37.3 14.7 %collective-permute-start.9 = (f32[1,32,128]{2,1,0:T(8,128)S(1)}, f32[1,32,128]{2,1,0:T(8,128)S(1)}, u32[]{:S(2)}, u32[]{:S(2)}) collective-permute-start(f32[1,32,128]{2,1,0:T(8,128)S(1)} %get-tuple-element.202), channel_id=1, source_target_pairs={{32,0},{64,32},{96,64},{128,96},{160,128},{192,160},{224,192},{256... | collective-permute-start | bytes 49160 | tf_op jit(solution)/shard_map/ppermute | solution.py:18
  39.3 59.3 %all-to-all-start.1 = ((f32[32,32,128]{2,1,0:T(8,128)}), f32[32,32,128]{2,1,0:T(8,128)S(1)}, u32[]{:S(2)}, u32[]{:S(2)}) async-start(f32[32,32,128]{2,1,0:T(8,128)} %param.7), calls=%async_computation.1 | async-start | bytes 1048576 | tf_op jit(solution)/shard_map/all_to_all | solution.py:109
  52.1 4.8 %collective-permute-start.10 = (f32[34,1,128]{2,1,0:T(1,128)S(1)}, f32[34,1,128]{2,1,0:T(1,128)S(1)}, u32[]{:S(2)}, u32[]{:S(2)}) collective-permute-start(f32[34,1,128]{2,1,0:T(1,128)S(1)} %get-tuple-element.111), channel_id=1, source_target_pairs={{0,1},{1,2},{2,3},{3,4},{4,5},{5,6},{6,7},{7,8},{8,9},{9,10},{10,1... | collective-permute-start | bytes 52232 | tf_op jit(solution)/shard_map/ppermute | solution.py:17
  54.3 4.2 %collective-permute-start.11 = (f32[34,1,128]{2,1,0:T(1,128)S(1)}, f32[34,1,128]{2,1,0:T(1,128)S(1)}, u32[]{:S(2)}, u32[]{:S(2)}) collective-permute-start(f32[34,1,128]{2,1,0:T(1,128)S(1)} %get-tuple-element.112), channel_id=1, source_target_pairs={{1,0},{2,1},{3,2},{4,3},{5,4},{6,5},{7,6},{8,7},{9,8},{10,9},{11,1... | collective-permute-start | bytes 52232 | tf_op jit(solution)/shard_map/ppermute | solution.py:18
  56.9 19.7 %copy-start.2 = (f32[31,32,128]{2,1,0:T(8,128)}, f32[31,32,128]{2,1,0:T(8,128)S(1)}, u32[]{:S(2)}) copy-start(f32[31,32,128]{2,1,0:T(8,128)S(1)} %add_multiply_fusion) | copy-start | bytes 1523716
  59.4 7.1 %collective-permute-start.12 = (f32[1,32,128]{2,1,0:T(8,128)S(1)}, f32[1,32,128]{2,1,0:T(8,128)S(1)}, u32[]{:S(2)}, u32[]{:S(2)}) collective-permute-start(f32[1,32,128]{2,1,0:T(8,128)S(1)} %get-tuple-element.199), channel_id=1, source_target_pairs={{0,32},{32,64},{64,96},{96,128},{128,160},{160,192},{192,224},{224... | collective-permute-start | bytes 49160 | tf_op jit(solution)/shard_map/ppermute | solution.py:17
  64.6 5.6 %collective-permute-start.13 = (f32[1,32,128]{2,1,0:T(8,128)S(1)}, f32[1,32,128]{2,1,0:T(8,128)S(1)}, u32[]{:S(2)}, u32[]{:S(2)}) collective-permute-start(f32[1,32,128]{2,1,0:T(8,128)S(1)} %get-tuple-element.200), channel_id=1, source_target_pairs={{32,0},{64,32},{96,64},{128,96},{160,128},{192,160},{224,192},{256... | collective-permute-start | bytes 49160 | tf_op jit(solution)/shard_map/ppermute | solution.py:18
  70.2 6.4 %collective-permute-start.14 = (f32[34,1,128]{2,1,0:T(1,128)S(1)}, f32[34,1,128]{2,1,0:T(1,128)S(1)}, u32[]{:S(2)}, u32[]{:S(2)}) collective-permute-start(f32[34,1,128]{2,1,0:T(1,128)S(1)} %get-tuple-element.109), channel_id=1, source_target_pairs={{0,1},{1,2},{2,3},{3,4},{4,5},{5,6},{6,7},{7,8},{8,9},{9,10},{10,1... | collective-permute-start | bytes 52232 | tf_op jit(solution)/shard_map/ppermute | solution.py:17
  74.3 3.1 %collective-permute-start.15 = (f32[34,1,128]{2,1,0:T(1,128)S(1)}, f32[34,1,128]{2,1,0:T(1,128)S(1)}, u32[]{:S(2)}, u32[]{:S(2)}) collective-permute-start(f32[34,1,128]{2,1,0:T(1,128)S(1)} %get-tuple-element.110), channel_id=1, source_target_pairs={{1,0},{2,1},{3,2},{4,3},{5,4},{6,5},{7,6},{8,7},{9,8},{10,9},{11,1... | collective-permute-start | bytes 52232 | tf_op jit(solution)/shard_map/ppermute | solution.py:18
  78.3 7.6 %collective-permute-start.16 = (f32[1,32,128]{2,1,0:T(8,128)S(1)}, f32[1,32,128]{2,1,0:T(8,128)S(1)}, u32[]{:S(2)}, u32[]{:S(2)}) collective-permute-start(f32[1,32,128]{2,1,0:T(8,128)S(1)} %get-tuple-element.197), channel_id=1, source_target_pairs={{0,32},{32,64},{64,96},{96,128},{128,160},{160,192},{192,224},{224... | collective-permute-start | bytes 49160 | tf_op jit(solution)/shard_map/ppermute | solution.py:17
  83.1 6.6 %collective-permute-start.17 = (f32[1,32,128]{2,1,0:T(8,128)S(1)}, f32[1,32,128]{2,1,0:T(8,128)S(1)}, u32[]{:S(2)}, u32[]{:S(2)}) collective-permute-start(f32[1,32,128]{2,1,0:T(8,128)S(1)} %get-tuple-element.198), channel_id=1, source_target_pairs={{32,0},{64,32},{96,64},{128,96},{160,128},{192,160},{224,192},{256... | collective-permute-start | bytes 49160 | tf_op jit(solution)/shard_map/ppermute | solution.py:18
  89.8 5.3 %collective-permute-start.18 = (f32[34,1,128]{2,1,0:T(1,128)S(1)}, f32[34,1,128]{2,1,0:T(1,128)S(1)}, u32[]{:S(2)}, u32[]{:S(2)}) collective-permute-start(f32[34,1,128]{2,1,0:T(1,128)S(1)} %get-tuple-element.107), channel_id=1, source_target_pairs={{0,1},{1,2},{2,3},{3,4},{4,5},{5,6},{6,7},{7,8},{8,9},{9,10},{10,1... | collective-permute-start | bytes 52232 | tf_op jit(solution)/shard_map/ppermute | solution.py:17
  93.0 3.8 %collective-permute-start.19 = (f32[34,1,128]{2,1,0:T(1,128)S(1)}, f32[34,1,128]{2,1,0:T(1,128)S(1)}, u32[]{:S(2)}, u32[]{:S(2)}) collective-permute-start(f32[34,1,128]{2,1,0:T(1,128)S(1)} %get-tuple-element.108), channel_id=1, source_target_pairs={{1,0},{2,1},{3,2},{4,3},{5,4},{6,5},{7,6},{8,7},{9,8},{10,9},{11,1... | collective-permute-start | bytes 52232 | tf_op jit(solution)/shard_map/ppermute | solution.py:18
  98.5 26.3 %all-to-all-start = ((f32[32,32,128]{2,1,0:T(8,128)}), f32[32,32,128]{2,1,0:T(8,128)S(1)}, u32[]{:S(2)}, u32[]{:S(2)}) async-start(f32[32,32,128]{2,1,0:T(8,128)} %fusion.11), calls=%async_computation | async-start | bytes 1048576 | tf_op jit(solution)/shard_map/all_to_all | solution.py:108
  125.4 1.0 copy-start.7
  125.4 1.2 copy-start.8
  134.1 5.5 %copy-start.3 = (f32[31,32,128]{2,1,0:T(8,128)S(1)}, f32[31,32,128]{2,1,0:T(8,128)}, u32[]{:S(2)}) copy-start(f32[31,32,128]{2,1,0:T(8,128)} %copy-done.2) | copy-start | bytes 1523716
  135.2 15.2 %all-to-all-start.2 = ((f32[1,1024,128]{2,0,1:T(1,128)}), f32[1,1024,128]{2,0,1:T(1,128)S(1)}, u32[]{:S(2)}, u32[]{:S(2)}) async-start(f32[1,1024,128]{2,0,1:T(1,128)} %bitcast.8), calls=%async_computation.2 | async-start | bytes 1048576 | tf_op jit(solution)/shard_map/all_to_all | solution.py:90
  150.4 1.0 copy-start.12
  152.0 1.0 copy-start.9
  152.0 1.2 copy-start.10
  152.0 1.3 copy-start.11
  159.3 6.9 %copy-start.5 = (f32[31,32,128]{2,1,0:T(8,128)}, f32[31,32,128]{2,1,0:T(8,128)S(1)}, u32[]{:S(2)}) copy-start(f32[31,32,128]{2,1,0:T(8,128)S(1)} %get-tuple-element.60) | copy-start | bytes 1523716
  159.9 6.4 %collective-permute-start.20 = (f32[3,32,128]{2,1,0:T(8,128)S(1)}, f32[3,32,128]{2,1,0:T(8,128)S(1)}, u32[]{:S(2)}, u32[]{:S(2)}) collective-permute-start(f32[3,32,128]{2,1,0:T(8,128)S(1)} %pad_maximum_fusion.15), channel_id=1, source_target_pairs={{32,0},{64,32},{96,64},{128,96},{160,128},{192,160},{224,192},{256... | collective-permute-start | bytes 147464 | tf_op jit(solution)/shard_map/ppermute | solution.py:26
  167.4 61.8 %all-to-all-start.3 = ((f32[16,1,4,32,128]{4,3,2,1,0:T(8,128)}), f32[16,1,4,32,128]{4,3,2,1,0:T(8,128)S(1)}, u32[]{:S(2)}, u32[]{:S(2)}) async-start(f32[16,1,4,32,128]{4,3,2,1,0:T(8,128)} %stack.31), calls=%async_computation.3 | async-start | bytes 2097152 | tf_op jit(solution)/shard_map/all_to_all | solution.py:151
  231.2 1.0 copy-start.6
